TPU v7x, 32 devices: a whole 2x2x4 slice. The times are simulated.
32 devices in a mesh: ctx: 8 (over z, y), grp: 4 (over x, core).
Axes of the slice: x: 2, y: 2, z: 4, core: 2. Of those that a mesh axis runs over, the one named last changes fastest.
Arguments:
- channels: bfloat16 [4096, 5120], P(('ctx', 'grp')), may hold values from -6 to 6
- gates: bfloat16 [4096, 5120], P(('ctx', 'grp')), may hold values from -6 to 6
- b_proj: bfloat16 [4096, 128], P(('ctx', 'grp')), may hold values from -6 to 6
- c_proj: bfloat16 [4096, 128], P(('ctx', 'grp')), may hold values from -0.5 to 0.5
- step_size: bfloat16 [4096, 80], P(('ctx', 'grp')), may hold values from 0.001 to 1, as said below
- log_decay: bfloat16 [4096, 80], P(('ctx', 'grp')), may hold values from -1 to 0, as said below
- skip_gain: float32 [80], P('grp'), may hold values from 0.5 to 2
- norm_gain: float32 [5120], P('grp'), may hold values from 0.1 to 1.9
- out_weight: bfloat16 [5120, 2560], P('grp'), may hold values from -0.078125 to 0.078125
Outputs:
- layer_out: bfloat16 [4096, 2560], P(('ctx', 'grp'))
Inputs may be any that keep to these rules, and one draw needn't show every extreme that they name: `step_size`: each token's step of each head is positive. `log_decay`: each token's log decay of each head is negative.
All inputs are finite; a program needn't handle non-finite values.
Results may differ from a plain program's by a relative error of at most 0.009.
Values may be sent and summed in bfloat16 or wider, within the bound.
A program may use at most 128 MiB of HBM per device.

v0:
```python
import jax
import jax.numpy as jnp
from jax import lax
from jax.sharding import PartitionSpec as P

HEADS = 80
HD = 64
NSTATE = 128
GROUP = 256


def prefix_2(value, axis, join, neutral):
    count, mine = (lax.axis_size(axis), lax.axis_index(axis))
    pieces = jax.tree.map(lambda part: lax.all_gather(part, axis), value)
    so_far = jax.tree.map(
        lambda part, zero: jnp.full_like(part, 0) + jnp.asarray(zero, part.dtype), value, neutral
    )

    def turn(position, so_far):
        longer = join(so_far, jax.tree.map(lambda part: part[position], pieces))
        return jax.tree.map(lambda new, old: jnp.where(position < mine, new, old), longer, so_far)

    return lax.fori_loop(0, count - 1, turn, so_far)


def local_scan(chan_heads, step_heads, decay_heads, b_rows, c_rows):
    highest = lax.Precision.HIGHEST
    piece_len = chan_heads.shape[0]
    nheads = step_heads.shape[1]
    blocks = piece_len // GROUP
    running = jnp.cumsum(decay_heads.astype(jnp.float32).reshape(blocks, GROUP, nheads), axis=1)
    running_t = jnp.transpose(running, (0, 2, 1))
    chan_f = chan_heads.astype(jnp.float32).reshape(piece_len, nheads, HD)
    inputs = (chan_f * step_heads.astype(jnp.float32)[:, :, None]).reshape(
        blocks, GROUP, nheads, HD
    )
    b_blocks = b_rows.reshape(blocks, GROUP, NSTATE)
    c_blocks = c_rows.reshape(blocks, GROUP, NSTATE)
    scores = jnp.einsum("qin,qjn->qij", c_blocks, b_blocks, preferred_element_type=jnp.float32)
    rows_at = lax.broadcasted_iota(jnp.int32, (GROUP, GROUP), 0)
    cols_at = lax.broadcasted_iota(jnp.int32, (GROUP, GROUP), 1)
    causal = rows_at >= cols_at
    spread = running_t[:, :, :, None] - running_t[:, :, None, :]
    weights = jnp.where(causal[None, None], jnp.exp(spread), 0.0) * scores[:, None]
    y_intra = jnp.einsum("qhij,qjhp->qihp", weights, inputs, precision=highest)
    tail_decay = jnp.exp(running[:, -1:, :] - running)
    b_float = b_blocks.astype(jnp.float32)
    c_float = c_blocks.astype(jnp.float32)
    group_states = jnp.einsum(
        "qjhp,qjn->qhpn", inputs * tail_decay[..., None], b_float, precision=highest
    )
    totals = jnp.exp(running[:, -1, :])

    def carry_step(carried, packed):
        factor, fresh_state = packed
        return (factor[:, None, None] * carried + fresh_state, carried)

    final_state, starts = lax.scan(
        carry_step, jnp.zeros((nheads, HD, NSTATE), jnp.float32), (totals, group_states)
    )
    y_inter = (
        jnp.einsum("qin,qhpn->qihp", c_float, starts, precision=highest)
        * jnp.exp(running)[..., None]
    )
    group_logs = running[:, -1, :]
    offsets = jnp.cumsum(group_logs, axis=0) - group_logs
    piece_cum = (running + offsets[:, None, :]).reshape(piece_len, nheads)
    piece_log = jnp.sum(group_logs, axis=0)
    local_out = (y_intra + y_inter).reshape(piece_len, nheads, HD)
    return (local_out, final_state, piece_log, piece_cum, chan_f)


def local(channels, gates, b_proj, c_proj, step_size, log_decay, skip_gain, norm_gain, out_weight):
    highest = lax.Precision.HIGHEST
    chan_heads, gate_heads, step_heads, decay_heads = (
        lax.all_to_all(channels, "grp", split_axis=1, concat_axis=0, tiled=True),
        lax.all_to_all(gates, "grp", split_axis=1, concat_axis=0, tiled=True),
        lax.all_to_all(step_size, "grp", split_axis=1, concat_axis=0, tiled=True),
        lax.all_to_all(log_decay, "grp", split_axis=1, concat_axis=0, tiled=True),
    )
    b_rows, c_rows = (
        lax.all_gather(b_proj, "grp", axis=0, tiled=True),
        lax.all_gather(c_proj, "grp", axis=0, tiled=True),
    )
    local_out, final_state, piece_log, piece_cum, chan_f = local_scan(
        chan_heads, step_heads, decay_heads, b_rows, c_rows
    )
    piece_factor = jnp.exp(piece_log)

    def combine(early_part, later_part):
        return (
            early_part[0] * later_part[0],
            later_part[0][:, None, None] * early_part[1] + later_part[1],
        )

    identity = (jnp.ones_like(piece_factor), jnp.zeros_like(final_state))
    prefix = prefix_2((piece_factor, final_state), "ctx", combine, identity)
    incoming = prefix[1]
    correction = jnp.einsum("tn,hpn->thp", c_rows.astype(jnp.float32), incoming, precision=highest)
    correction = correction * jnp.exp(piece_cum)[:, :, None]
    ssm_out = local_out + correction + skip_gain[None, :, None] * chan_f
    piece_len = chan_heads.shape[0]
    gated_out = ssm_out.reshape(piece_len, chan_heads.shape[1]) * jax.nn.silu(
        gate_heads.astype(jnp.float32)
    )
    row_squares = lax.psum(jnp.sum(gated_out * gated_out, axis=1), "grp")
    scale = lax.rsqrt(row_squares / (HEADS * HD) + 1e-05)
    normed = (gated_out * scale[:, None] * norm_gain[None, :]).astype(jnp.bfloat16)
    return lax.psum_scatter(
        jnp.dot(normed, out_weight, preferred_element_type=jnp.float32).astype(jnp.bfloat16),
        "grp",
        scatter_dimension=0,
        tiled=True,
    )


def solution(mesh):
    in_specs = (
        P(("ctx", "grp"), None),
        P(("ctx", "grp"), None),
        P(("ctx", "grp"), None),
        P(("ctx", "grp"), None),
        P(("ctx", "grp"), None),
        P(("ctx", "grp"), None),
        P("grp"),
        P("grp"),
        P("grp", None),
    )
    out_specs = P(("ctx", "grp"), None)
    return jax.shard_map(local, mesh=mesh, in_specs=in_specs, out_specs=out_specs, check_vma=False)
```

profile of v0, /device:TPU:0, one launch (start us, length us, event | category | flops | bytes accessed | tf_op | source)
XLA Modules:
  0.0 233.1 jit_solution(6459703165636211416)
XLA Ops:
  6.5 1.4 all_to_all.44
  7.9 4.2 %all-to-all-start.2 = ((bf16[128,4,20]{0,2,1:T(8,128)(2,1)}), bf16[128,4,20]{0,2,1:T(8,128)(2,1)S(1)}, u32[]{:S(2)}, u32[]{:S(2)}) async-start(bf16[128,4,20]{0,2,1:T(8,128)(2,1)} %all_to_all.44), calls=%async_computation.2 | async-start | bytes 49152 | tf_op jit(solution)/shard_map/all_to_all | solution.py:79
  12.1 5.8 %all_gather.17 = bf16[512,128]{1,0:T(8,128)(2,1)S(1)} all-gather(bf16[128,128]{1,0:T(8,128)(2,1)} %param.15), channel_id=1, replica_groups=mesh['ctx'=8,'grp'=4] {'grp'}, dimensions={0}, use_global_device_ids=true | all-gather | bytes 163840 | tf_op jit(solution)/shard_map/all_gather | solution.py:82
  17.9 2.4 %copy.51 = bf16[128,5120]{0,1:T(8,128)(2,1)} copy(bf16[128,5120]{1,0:T(8,128)(2,1)} %param.13) | data formatting | bytes 2621440 | tf_op args[0]
  20.9 3.3 %all-to-all-start.1 = ((bf16[128,4,20]{0,2,1:T(8,128)(2,1)}), bf16[128,4,20]{0,2,1:T(8,128)(2,1)S(1)}, u32[]{:S(2)}, u32[]{:S(2)}) async-start(bf16[128,4,20]{0,2,1:T(8,128)(2,1)} %all_to_all.42), calls=%async_computation.1 | async-start | bytes 49152 | tf_op jit(solution)/shard_map/all_to_all | solution.py:78
  24.3 1.2 reduce-window.6
  25.7 2.3 %all-to-all-done.1 = bf16[128,4,20]{0,2,1:T(8,128)(2,1)S(1)} async-done(((bf16[128,4,20]{0,2,1:T(8,128)(2,1)}), bf16[128,4,20]{0,2,1:T(8,128)(2,1)S(1)}, u32[]{:S(2)}, u32[]{:S(2)}) %all-to-all-start.1) | async-done | bytes 20512 | tf_op jit(solution)/shard_map/all_to_all | solution.py:78
  28.1 3.5 %all-to-all-start = ((bf16[128,4,1280]{0,2,1:T(8,128)(2,1)}), bf16[128,4,1280]{0,2,1:T(8,128)(2,1)S(1)}, u32[]{:S(2)}, u32[]{:S(2)}) async-start(bf16[128,4,1280]{0,2,1:T(8,128)(2,1)} %bitcast), calls=%async_computation | async-start | bytes 2621440 | tf_op jit(solution)/shard_map/all_to_all | solution.py:76
  33.5 15.3 %all-to-all-done = bf16[128,4,1280]{0,2,1:T(8,128)(2,1)S(1)} async-done(((bf16[128,4,1280]{0,2,1:T(8,128)(2,1)}), bf16[128,4,1280]{0,2,1:T(8,128)(2,1)S(1)}, u32[]{:S(2)}, u32[]{:S(2)}) %all-to-all-start) | async-done | bytes 1310752 | tf_op jit(solution)/shard_map/all_to_all | solution.py:76
  49.0 5.4 %copy.52 = f32[4,128,1280]{1,0,2:T(4,128)S(1)} copy(f32[4,128,1280]{1,2,0:T(8,128)S(1)} %convert_bitcast_fusion.1) | data formatting | bytes 5242880 | tf_op jit(solution)/shard_map/convert_element_type | solution.py:33
  54.5 3.3 %reshape.122 = f32[2,256,20,64]{1,0,3,2:T(2,128)} reshape(f32[4,128,1280]{1,0,2:T(4,128)S(1)} %copy.52) | data formatting | bytes 5242880 | tf_op jit(solution)/shard_map/convert_element_type | solution.py:33
  57.8 5.1 %broadcast_multiply_fusion = (f32[2,256,20,64]{1,0,3,2:T(2,128)S(1)}, f32[2,256,20,64]{1,0,3,2:T(2,128)}) fusion(f32[2,256,20]{1,0,2:T(2,128)S(1)} %get-tuple-element.189, f32[2,256,20,64]{1,0,3,2:T(2,128)} %reshape.122, f32[2,256,20]{1,0,2:T(2,128)S(1)} %reshape.123), kind=kLoop, calls=%fused_computation.39 | loop fusion | flops 1310720 | bytes 7946240 | tf_op jit(solution)/shard_map/mul | solution.py:50
  62.9 2.4 %fusion.22 = f32[2,20,64,128]{3,2,1,0:T(8,128)} fusion(bf16[2,256,128,1]{2,1,3,0:T(8,128)(2,1)S(1)} %bitcast.131, f32[2,256,20,64]{1,0,3,2:T(2,128)S(1)} %get-tuple-element.186), kind=kOutput, calls=%fused_computation.33 | convolution fusion | flops 1006632960 | bytes 4063232 | tf_op jit(solution)/shard_map/qjhp,qjn->qhpn/dot_general | solution.py:49
  65.3 4.3 %while.27 = (s32[]{:T(128)}, f32[20,64,128]{2,1,0:T(8,128)S(1)}, f32[2,20,64,128]{3,2,1,0:T(8,128)}, f32[2,20]{1,0:T(2,128)S(1)}, f32[2,20,64,128]{3,2,1,0:T(8,128)}, /*index=5*/s32[]{:T(128)}, s32[]{:T(128)}) while((s32[]{:T(128)}, f32[20,64,128]{2,1,0:T(8,128)S(1)}, f32[2,20,64,128]{3,2,1,0:T(8,128)}, f32[2,20]{1,0:T(2,128)S(1)}, ...), condition=%wide.region_3.4_spmd.clone, body=%wide.region_2.3_spmd.clone.sunk | while | flops 655363 | bytes 3277648 | solution.py:58
  65.3 0.9 bitcast_dynamic-update-slice_fusion.2
  66.2 1.2 bitcast_add_fusion.3
  67.5 0.9 bitcast_dynamic-update-slice_fusion.2
  68.4 1.2 bitcast_add_fusion.3
  69.6 0.8 copy-done
  70.5 2.5 %copy.68 = bf16[128,5120]{0,1:T(8,128)(2,1)} copy(bf16[128,5120]{1,0:T(8,128)(2,1)} %param.14) | data formatting | bytes 2621440 | tf_op args[1]
  72.9 4.3 %all-to-all-start.3 = ((bf16[128,4,1280]{0,2,1:T(8,128)(2,1)}), bf16[128,4,1280]{0,2,1:T(8,128)(2,1)}, u32[]{:S(2)}, u32[]{:S(2)}) async-start(bf16[128,4,1280]{0,2,1:T(8,128)(2,1)} %bitcast.127), calls=%async_computation.3 | async-start | bytes 2621440 | tf_op jit(solution)/shard_map/all_to_all | solution.py:77
  78.5 17.5 %all_gather.16 = bf16[512,128]{1,0:T(8,128)(2,1)S(1)} all-gather(bf16[128,128]{1,0:T(8,128)(2,1)} %param.16), channel_id=1, replica_groups=mesh['ctx'=8,'grp'=4] {'grp'}, dimensions={0}, use_global_device_ids=true | all-gather | bytes 163840 | tf_op jit(solution)/shard_map/all_gather | solution.py:83
  96.7 1.0 fusion.28
  97.7 1.4 copy.57
  100.0 22.7 %all-reduce = f32[160]{0:T(256)S(1)} all-reduce(f32[160]{0:T(256)S(1)} %exponential_dynamic-update-slice_fusion), channel_id=2, replica_groups=mesh['ctx'=8,'grp'=4] {'ctx'}, use_global_device_ids=true, to_apply=%add | all-reduce | flops 160 | bytes 1280
  124.2 2.1 reshape.125
  126.3 13.1 %fusion.2 = f32[2,20,64,256]{3,2,1,0:T(8,128)S(1)} fusion(f32[2,256,256]{2,1,0:T(8,128)} %fusion.28, f32[2,20,256]{2,1,0:T(8,128)} %copy.57, pred[256,256]{1,0:T(8,128)(4,1)S(1)} %copy-done.3, f32[2,256,20,64]{1,0,3,2:T(2,128)} %get-tuple-element.187), kind=kOutput, calls=%fused_computation.7 | convolution fusion | flops 2021130240 | bytes 5873664 | tf_op jit(solution)/shard_map/qhij,qjhp->qihp/dot_general | solution.py:45
  139.5 1.3 fusion.21
  140.9 1.9 copy.74
  142.7 1.6 copy.69
  144.3 1.7 convert_bitcast_fusion
  146.1 4.1 %copy.71 = f32[4,128,1280]{1,0,2:T(4,128)} copy(f32[4,128,1280]{2,1,0:T(8,128)} %convert_bitcast_fusion) | data formatting | bytes 5242880 | tf_op jit(solution)/shard_map/convert_element_type | solution.py:104
  150.2 4.1 %reshape.127 = f32[512,20,64]{0,2,1:T(8,128)} reshape(f32[4,128,1280]{1,0,2:T(4,128)} %copy.71) | data formatting | bytes 5242880 | tf_op jit(solution)/shard_map/convert_element_type | solution.py:104
  154.4 3.5 %all-gather.4.cloned.1.call-done = f32[160,64,128]{2,1,0:T(8,128)} async-done(((f32[20,64,128]{2,1,0:T(8,128)}), f32[160,64,128]{2,1,0:T(8,128)}) %all-gather.4.cloned.1.call-update) | async-done | bytes 5242896 | tf_op jit(solution)/shard_map/all_gather | solution.py:14
  157.9 8.9 %while.28 = (s32[]{:T(128)}, f32[20,64,128]{2,1,0:T(8,128)S(1)}, s32[]{:T(128)}, f32[8,20]{1,0:T(8,128)S(1)}, f32[8,20,64,128]{3,2,1,0:T(8,128)}, /*index=5*/s32[]{:T(128)}, s32[]{:T(128)}) while((s32[]{:T(128)}, f32[20,64,128]{2,1,0:T(8,128)S(1)}, s32[]{:T(128)}, f32[8,20]{1,0:T(8,128)S(1)}, f32[8,20,64,128]{3,2,1,0:T(8,128)}, ...), condition=%wide.region_6.7_spmd.clone, body=%wide.region_5.6_spmd.clone.sunk | while | flops 655364 | bytes 1966425 | solution.py:23
  157.9 1.2 fusion.40
  159.2 1.2 fusion.40
  160.5 1.2 fusion.40
  161.7 1.2 fusion.40
  163.0 1.2 fusion.40
  164.3 1.2 fusion.40
  165.6 1.2 fusion.40
  166.8 6.9 %multiply_reduce_fusion = (f32[512]{0:T(512)S(1)}, f32[512,20,64]{0,2,1:T(8,128)}) fusion(f32[512,20,64]{0,2,1:T(8,128)} %reshape.127, f32[512,20,64]{0,2,1:T(8,128)} %reshape.125, f32[20]{0:T(128)S(1)} %copy-done.7, f32[512,20,64]{0,2,1:T(8,128)} %bitcast.128, f32[512,20]{0,1:T(8,128)S(1)} %bitcast.139, f32[20,64,128]{2,1,0:T(8,128)S(1)} %get-tuple-element.129, ...), kind=kOutput, calls=%fused_computation.37 | convolution fusion | flops 1013841408 | bytes 11315280 | tf_op jit(solution)/shard_map/tn,hpn->thp/dot_general | solution.py:99
  173.7 3.2 %copy.70 = f32[512,1280]{1,0:T(8,128)} copy(f32[512,1280]{0,1:T(8,128)} %bitcast.129) | data formatting | bytes 5242880 | tf_op jit(solution)/shard_map/reshape | solution.py:103
  176.9 5.9 %psum.7 = f32[512]{0:T(512)S(1)} all-reduce(f32[512]{0:T(512)S(1)} %get-tuple-element.193), channel_id=1, replica_groups=mesh['ctx'=8,'grp'=4] {'grp'}, use_global_device_ids=true, to_apply=%region_9.10 | all-reduce | flops 512 | bytes 4096 | tf_op jit(solution)/shard_map/psum | solution.py:106
  182.9 2.6 %fusion.25 = bf16[512,1280]{1,0:T(8,128)(2,1)S(1)} fusion(f32[512,1280]{1,0:T(8,128)} %copy.70, bf16[128,4,1280]{2,0,1:T(8,128)(2,1)S(1)} %copy.69, f32[1280]{0:T(1024)S(1)} %copy-done.6, f32[512]{0:T(512)S(1)} %add_rsqrt_fusion), kind=kLoop, calls=%fused_computation.38 | loop fusion | flops 5898240 | bytes 5250048 | tf_op jit(solution)/shard_map/convert_element_type | solution.py:108
  185.5 7.7 %convolution_convert_fusion = bf16[512,2560]{1,0:T(8,128)(2,1)} fusion(bf16[512,1280]{1,0:T(8,128)(2,1)S(1)} %fusion.25, bf16[1280,2560]{1,0:T(8,128)(2,1)} %param.21), kind=kOutput, calls=%fused_computation.17 | convolution fusion | flops 3356753920 | bytes 10485760 | tf_op jit(solution)/shard_map/dot_general | solution.py:110
  193.2 33.1 %reduce-scatter.2.cloned.1.call-done = bf16[128,2560]{1,0:T(8,128)(2,1)} async-done(((bf16[512,2560]{1,0:T(8,128)(2,1)}), bf16[128,2560]{1,0:T(8,128)(2,1)}) %reduce-scatter.2.cloned.1.call-update) | async-done | bytes 655376 | tf_op jit(solution)/shard_map/reduce_scatter | solution.py:109
  (69 shorter events, 6.7 us)
Async XLA Ops:
  6.5 13.8 %copy-start.5 = (bf16[128,80]{0,1:T(8,128)(2,1)S(1)}, bf16[128,80]{0,1:T(8,128)(2,1)}, u32[]{:S(2)}) copy-start(bf16[128,80]{0,1:T(8,128)(2,1)} %param.17) | copy-start | bytes 61444
  7.9 13.0 %all-to-all-start.2 = ((bf16[128,4,20]{0,2,1:T(8,128)(2,1)}), bf16[128,4,20]{0,2,1:T(8,128)(2,1)S(1)}, u32[]{:S(2)}, u32[]{:S(2)}) async-start(bf16[128,4,20]{0,2,1:T(8,128)(2,1)} %all_to_all.44), calls=%async_computation.2 | async-start | bytes 49152 | tf_op jit(solution)/shard_map/all_to_all | solution.py:79
  20.9 7.1 %all-to-all-start.1 = ((bf16[128,4,20]{0,2,1:T(8,128)(2,1)}), bf16[128,4,20]{0,2,1:T(8,128)(2,1)S(1)}, u32[]{:S(2)}, u32[]{:S(2)}) async-start(bf16[128,4,20]{0,2,1:T(8,128)(2,1)} %all_to_all.42), calls=%async_computation.1 | async-start | bytes 49152 | tf_op jit(solution)/shard_map/all_to_all | solution.py:78
  28.1 20.8 %all-to-all-start = ((bf16[128,4,1280]{0,2,1:T(8,128)(2,1)}), bf16[128,4,1280]{0,2,1:T(8,128)(2,1)S(1)}, u32[]{:S(2)}, u32[]{:S(2)}) async-start(bf16[128,4,1280]{0,2,1:T(8,128)(2,1)} %bitcast), calls=%async_computation | async-start | bytes 2621440 | tf_op jit(solution)/shard_map/all_to_all | solution.py:76
  31.6 126.3 %all-gather.4.cloned.1.call-start = ((), (), s32[]{:S(2)}) async-start(), calls=%async_computation.6 | async-start | bytes 5898240 | tf_op jit(solution)/shard_map/all_gather | solution.py:14
  31.8 17.0 %copy-start.2 = (f32[2,20,256]{2,0,1:T(2,128)}, f32[2,20,256]{2,0,1:T(2,128)S(1)}, u32[]{:S(2)}) copy-start(f32[2,20,256]{2,0,1:T(2,128)S(1)} %reduce_window_sum.35) | copy-start | bytes 122884
  69.6 0.8 copy-start
  70.5 6.9 %copy-start.8 = (u32[32]{0:T(128)S(1)}, u32[32]{0:T(128)}, u32[]{:S(2)}) copy-start(u32[32]{0:T(128)} %constant.61) | copy-start | bytes 388
  72.9 69.8 %all-to-all-start.3 = ((bf16[128,4,1280]{0,2,1:T(8,128)(2,1)}), bf16[128,4,1280]{0,2,1:T(8,128)(2,1)}, u32[]{:S(2)}, u32[]{:S(2)}) async-start(bf16[128,4,1280]{0,2,1:T(8,128)(2,1)} %bitcast.127), calls=%async_computation.3 | async-start | bytes 2621440 | tf_op jit(solution)/shard_map/all_to_all | solution.py:77
  77.3 149.0 %reduce-scatter.2.cloned.1.call-start = ((), (), s32[]{:S(2)}) async-start(), calls=%async_computation.5 | async-start | bytes 3276800 | tf_op jit(solution)/shard_map/reduce_scatter | solution.py:109
  124.2 2.1 copy-start.3
  126.3 13.1 %copy-start.1 = (f32[2,20,64,128]{3,2,1,0:T(8,128)S(1)}, f32[2,20,64,128]{3,2,1,0:T(8,128)}, u32[]{:S(2)}) copy-start(f32[2,20,64,128]{3,2,1,0:T(8,128)} %get-tuple-element.127) | copy-start | bytes 3932164
  157.9 8.9 %copy-start.4 = (f32[3,8,2,256]{3,1,2,0:T(8,128)S(1)}, f32[3,8,2,256]{3,1,2,0:T(8,128)}, u32[]{:S(2)}) copy-start(f32[3,8,2,256]{3,1,2,0:T(8,128)} %copy.75) | copy-start | bytes 147460
  157.9 8.9 %copy-start.7 = (f32[20]{0:T(128)S(1)}, f32[20]{0:T(128)}, u32[]{:S(2)}) copy-start(f32[20]{0:T(128)} %param.19) | copy-start | bytes 244
  173.7 9.2 %copy-start.6 = (f32[1280]{0:T(1024)S(1)}, f32[1280]{0:T(1024)}, u32[]{:S(2)}) copy-start(f32[1280]{0:T(1024)} %param.20) | copy-start | bytes 15364
Sparse Core Ops, SparseCore 0:
  70.6 87.2 all-gather.3
  193.3 32.9 reduce-scatter.1
where the time goes:
time: 235 us; the launch traced here: 233 us
  waiting for transfers between devices  54.3 us (23%)
  blocking collectives  51.9 us (22%)
  local copies, waits for them, and re-layouts  38.9 us (17%)
  matrix products  32.5 us (14%)
  other arithmetic  25.6 us (11%)
  starting transfers between devices  15.4 us (7%)
  between operations  14.3 us (6%)
    reduce_scatter x1, waiting for transfers between devices, local(): lax.psum_scatter(jnp.dot(normed, out_weight, preferred_element_type=jnp.f...  33.1 us
    unnamed x1, blocking collectives  22.7 us
    all_gather x1, blocking collectives, local(): lax.all_gather(c_proj, 'grp', axis=0, tiled=True)  17.5 us
    all_to_all x1, waiting for transfers between devices, local(): lax.all_to_all(channels, 'grp', split_axis=1, concat_axis=0, tiled=True)  15.3 us
    dot_general x1, matrix products, local_scan(): y_intra = jnp.einsum('qhij,qjhp->qihp', weights, inputs, precision=highest)  13.1 us
    convert_element_type x3, local copies, waits for them, and re-layouts, local_scan(): chan_f = chan_heads.astype(jnp.float32).reshape(piece_len, nheads, HD)  10.9 us
    select_n x7, other arithmetic, turn(): jnp.where(position < mine, new, old)  8.64 us
    convert_element_type x2, local copies, waits for them, and re-layouts, local(): gate_heads.astype(jnp.float32)  8.27 us
  transfers between devices with their start and end apart: 6, of which 4 were waited for; matrix products, arithmetic and copies ran while one was open for 19% of the time, Pallas kernels for 0%

commit v1 on v0

--- a/solution.py
+++ b/solution.py
@@ -7,6 +7,22 @@
 HD = 64
 NSTATE = 128
 GROUP = 256
+
+
+def exchange_in_pairs(x, axis, split, join):
+    ways, here = (lax.axis_size(axis), lax.axis_index(axis))
+    width = x.shape[split] // ways
+    shape = list(x.shape)
+    shape[split] = width
+    height = shape[join]
+    shape[join] = height * ways
+    full = jnp.zeros(shape, x.dtype)
+    for mask in range(ways):
+        part = lax.dynamic_slice_in_dim(x, (here ^ mask) * width, width, axis=split)
+        if mask:
+            part = lax.ppermute(part, axis, [(d, d ^ mask) for d in range(ways)])
+        full = lax.dynamic_update_slice_in_dim(full, part, (here ^ mask) * height, axis=join)
+    return full
 
 
 def prefix_2(value, axis, join, neutral):
@@ -73,7 +89,7 @@
 def local(channels, gates, b_proj, c_proj, step_size, log_decay, skip_gain, norm_gain, out_weight):
     highest = lax.Precision.HIGHEST
     chan_heads, gate_heads, step_heads, decay_heads = (
-        lax.all_to_all(channels, "grp", split_axis=1, concat_axis=0, tiled=True),
+        exchange_in_pairs(channels, "grp", 1, 0),
         lax.all_to_all(gates, "grp", split_axis=1, concat_axis=0, tiled=True),
         lax.all_to_all(step_size, "grp", split_axis=1, concat_axis=0, tiled=True),
         lax.all_to_all(log_decay, "grp", split_axis=1, concat_axis=0, tiled=True),

time: 235 us -> 223 us (0.949)
  waiting for transfers between devices: 54.3 us -> 42 us
  matrix products: 32.5 us -> 23.8 us
  blocking collectives: 51.9 us -> 58.5 us
  other arithmetic: 25.6 us -> 31.3 us
    all_to_all x1 -> x0, waiting for transfers between devices: 15.3 us -> none  [local(): lax.all_to_all(channels, 'grp', split_axis=1, concat_axis=0, tiled=True)]
    convert_element_type x3 -> x0, local copies, waits for them, and re-layouts: 10.9 us -> none  [local_scan(): chan_f = chan_heads.astype(jnp.float32).reshape(piece_len, nheads, HD)]
    all_gather x1, blocking collectives: 5.76 us -> 12.8 us  [local(): lax.all_gather(b_proj, 'grp', axis=0, tiled=True)]
    reduce_sum x0 -> x2, other arithmetic: none -> 6.54 us  [the longest x1 5.65 us: local(): row_squares = lax.psum(jnp.sum(gated_out * gated_out, axis=1), 'grp')]
    dot_general x1, matrix products: 6.88 us -> 1.21 us  [local(): jnp.einsum('tn,hpn->thp', c_rows.astype(jnp.float32), incoming, precision...]
    all_gather x1, waiting for transfers between devices: 3.54 us -> 8.55 us  [prefix_2(): pieces = jax.tree.map(lambda part: lax.all_gather(part, axis), value)]
    mul x7, local copies, waits for them, and re-layouts: 0.05 us -> 4.83 us  [combine(): later_part[0][:, None, None] * early_part[1] + later_part[1]]
    all_to_all x1 -> x0, starting transfers between devices: 3.54 us -> none  [local(): lax.all_to_all(channels, 'grp', split_axis=1, concat_axis=0, tiled=True)]
  transfers between devices with their start and end apart: 6 -> 8, of which waited for: 4 -> 2; matrix products, arithmetic and copies ran while one was open for 19% -> 19% of each run, Pallas kernels for 0% -> 0%
where the time goes in v1:
time: 223 us; the launch traced here: 221 us
  blocking collectives  58.5 us (26%)
  waiting for transfers between devices  42 us (19%)
  local copies, waits for them, and re-layouts  37.6 us (17%)
  other arithmetic  31.3 us (14%)
  matrix products  23.8 us (11%)
  between operations  14.4 us (6%)
  starting transfers between devices  13.3 us (6%)
    reduce_scatter x1, waiting for transfers between devices, local(): lax.psum_scatter(jnp.dot(normed, out_weight, preferred_element_type=jnp.f...  33.4 us
    unnamed x1, blocking collectives  22.5 us
    all_gather x1, blocking collectives, local(): lax.all_gather(c_proj, 'grp', axis=0, tiled=True)  17.5 us
    all_gather x1, blocking collectives, local(): lax.all_gather(b_proj, 'grp', axis=0, tiled=True)  12.8 us
    dot_general x1, matrix products, local_scan(): y_intra = jnp.einsum('qhij,qjhp->qihp', weights, inputs, precision=highest)  11.2 us
    select_n x7, other arithmetic, turn(): jnp.where(position < mine, new, old)  8.6 us
    all_gather x1, waiting for transfers between devices, prefix_2(): pieces = jax.tree.map(lambda part: lax.all_gather(part, axis), value)  8.55 us
    convert_element_type x2, local copies, waits for them, and re-layouts, local(): gate_heads.astype(jnp.float32)  8.33 us
  transfers between devices with their start and end apart: 8, of which 2 were waited for; matrix products, arithmetic and copies ran while one was open for 19% of the time, Pallas kernels for 0%

profile of v1, /device:TPU:0, one launch (start us, length us, event | category | flops | bytes accessed | tf_op | source)
XLA Modules:
  0.0 221.1 jit_solution(14201718586056240225)
XLA Ops:
  6.5 1.4 constant_dynamic-slice_fusion.1
  8.4 2.6 %collective-permute-start.1 = (bf16[128,1280]{1,0:T(8,128)(2,1)S(1)}, bf16[128,1280]{1,0:T(8,128)(2,1)}, u32[]{:S(2)}, u32[]{:S(2)}) collective-permute-start(bf16[128,1280]{1,0:T(8,128)(2,1)S(1)} %get-tuple-element.193), channel_id=1, source_target_pairs={{0,2},{1,3},{2,0},{3,1},{4,6},{5,7},{6,4},{7,5},{8,10},{9,11},{10,... | collective-permute-start | bytes 983048 | tf_op jit(solution)/shard_map/ppermute | solution.py:23
  11.7 3.3 %all-to-all-start.1 = ((bf16[128,4,20]{0,2,1:T(8,128)(2,1)}), bf16[128,4,20]{0,2,1:T(8,128)(2,1)S(1)}, u32[]{:S(2)}, u32[]{:S(2)}) async-start(bf16[128,4,20]{0,2,1:T(8,128)(2,1)} %all_to_all.32), calls=%async_computation.1 | async-start | bytes 49152 | tf_op jit(solution)/shard_map/all_to_all | solution.py:95
  15.4 12.8 %all_gather.17 = bf16[512,128]{1,0:T(8,128)(2,1)S(1)} all-gather(bf16[128,128]{1,0:T(8,128)(2,1)S(1)} %copy-done.8), channel_id=1, replica_groups=mesh['ctx'=8,'grp'=4] {'grp'}, dimensions={0}, use_global_device_ids=true | all-gather | bytes 163840 | tf_op jit(solution)/shard_map/all_gather | solution.py:98
  28.7 3.3 %all-to-all-start = ((bf16[128,4,20]{0,2,1:T(8,128)(2,1)}), bf16[128,4,20]{0,2,1:T(8,128)(2,1)S(1)}, u32[]{:S(2)}, u32[]{:S(2)}) async-start(bf16[128,4,20]{0,2,1:T(8,128)(2,1)} %all_to_all.30), calls=%async_computation | async-start | bytes 49152 | tf_op jit(solution)/shard_map/all_to_all | solution.py:94
  32.2 1.2 reduce-window.6
  34.0 0.9 slice_reduce_fusion.1
  36.1 1.2 copy.59
  37.3 1.2 copy.60
  38.6 1.2 copy.61
  39.9 2.7 %reshape.112 = f32[2,256,20,64]{1,0,3,2:T(2,128)} reshape(bf16[512,1280]{0,1:T(8,128)(2,1)S(1)} %constant_dynamic-update-slice_fusion) | data formatting | bytes 3932160 | tf_op jit(solution)/shard_map/reshape | solution.py:49
  42.6 5.1 %broadcast_multiply_fusion = (f32[2,256,20,64]{1,0,3,2:T(2,128)S(1)}, f32[2,256,20,64]{1,0,3,2:T(2,128)}) fusion(f32[2,256,20]{1,0,2:T(2,128)S(1)} %copy-done.6, f32[2,256,20,64]{1,0,3,2:T(2,128)} %reshape.112, f32[2,256,20]{1,0,2:T(2,128)S(1)} %reshape.120), kind=kLoop, calls=%fused_computation.38 | loop fusion | flops 1310720 | bytes 7946240 | tf_op jit(solution)/shard_map/mul | solution.py:66
  47.7 1.3 fusion.22
  49.0 2.1 while.27
  49.0 0.9 bitcast_dynamic-update-slice_fusion.2
  50.1 0.9 bitcast_dynamic-update-slice_fusion.2
  51.2 0.8 copy-done
  52.0 2.4 %copy.76 = bf16[128,5120]{0,1:T(8,128)(2,1)} copy(bf16[128,5120]{1,0:T(8,128)(2,1)} %param.14) | data formatting | bytes 2621440 | tf_op args[1]
  54.4 3.5 %all-to-all-start.2 = ((bf16[128,4,1280]{0,2,1:T(8,128)(2,1)}), bf16[128,4,1280]{0,2,1:T(8,128)(2,1)S(1)}, u32[]{:S(2)}, u32[]{:S(2)}) async-start(bf16[128,4,1280]{0,2,1:T(8,128)(2,1)} %bitcast.125), calls=%async_computation.2 | async-start | bytes 2621440 | tf_op jit(solution)/shard_map/all_to_all | solution.py:93
  59.2 17.5 %all_gather.16 = bf16[512,128]{1,0:T(8,128)(2,1)S(1)} all-gather(bf16[128,128]{1,0:T(8,128)(2,1)} %param.16), channel_id=1, replica_groups=mesh['ctx'=8,'grp'=4] {'grp'}, dimensions={0}, use_global_device_ids=true | all-gather | bytes 163840 | tf_op jit(solution)/shard_map/all_gather | solution.py:99
  77.4 1.0 fusion.30
  78.4 0.8 copy.66
  79.2 0.8 copy.72
  80.8 22.5 %all-reduce = f32[160]{0:T(256)S(1)} all-reduce(f32[160]{0:T(256)S(1)} %exponential_dynamic-update-slice_fusion), channel_id=2, replica_groups=mesh['ctx'=8,'grp'=4] {'ctx'}, use_global_device_ids=true, to_apply=%add | all-reduce | flops 160 | bytes 1280
  104.0 0.9 pad
  104.9 1.8 convert_element_type.49
  106.8 11.2 %fusion.2 = f32[2,20,64,256]{3,2,1,0:T(8,128)S(1)} fusion(f32[2,256,256]{2,1,0:T(8,128)S(1)} %copy-done.5, f32[2,20,256]{2,1,0:T(8,128)S(1)} %copy.66, pred[256,256]{1,0:T(8,128)(4,1)S(1)} %copy-done.7, f32[2,256,20,64]{1,0,3,2:T(2,128)S(1)} %copy-done.2), kind=kOutput, calls=%fused_computation.7 | convolution fusion | flops 2021130240 | bytes 5873664 | tf_op jit(solution)/shard_map/qhij,qjhp->qihp/dot_general | solution.py:61
  118.0 1.3 fusion.21
  119.4 1.9 copy.82
  121.9 1.8 convert_bitcast_fusion
  123.6 4.2 %copy.79 = f32[4,128,1280]{1,0,2:T(4,128)} copy(f32[4,128,1280]{2,1,0:T(8,128)} %convert_bitcast_fusion) | data formatting | bytes 5242880 | tf_op jit(solution)/shard_map/convert_element_type | solution.py:120
  127.8 4.1 %reshape.123 = f32[512,20,64]{0,2,1:T(8,128)} reshape(f32[4,128,1280]{1,0,2:T(4,128)} %copy.79) | data formatting | bytes 5242880 | tf_op jit(solution)/shard_map/convert_element_type | solution.py:120
  132.0 8.6 %all-gather.4.cloned.1.call-done = f32[160,64,128]{2,1,0:T(8,128)} async-done(((f32[20,64,128]{2,1,0:T(8,128)}), f32[160,64,128]{2,1,0:T(8,128)}) %all-gather.4.cloned.1.call-update) | async-done | bytes 5242896 | tf_op jit(solution)/shard_map/all_gather | solution.py:30
  140.5 13.8 %while.28 = (s32[]{:T(128)}, f32[20,64,128]{2,1,0:T(8,128)S(1)}, s32[]{:T(128)}, f32[8,20]{1,0:T(8,128)}, f32[8,20,64,128]{3,2,1,0:T(8,128)}, /*index=5*/s32[]{:T(128)}, s32[]{:T(128)}) while((s32[]{:T(128)}, f32[20,64,128]{2,1,0:T(8,128)S(1)}, s32[]{:T(128)}, f32[8,20]{1,0:T(8,128)}, f32[8,20,64,128]{3,2,1,0:T(8,128)}, ...), condition=%wide.region_6.7_spmd.clone, body=%wide.region_5.6_spmd.clone.sunk | while | flops 655364 | bytes 1966425 | solution.py:39
  141.2 1.2 fusion.42
  143.1 1.2 fusion.42
  145.1 1.2 fusion.42
  147.0 1.2 fusion.42
  149.0 1.2 fusion.42
  150.9 1.2 fusion.42
  152.8 1.2 fusion.42
  154.3 1.2 fusion.26
  156.0 5.6 %multiply_reduce_fusion = (f32[512]{0:T(512)S(1)}, f32[512,20,64]{0,2,1:T(8,128)}) fusion(f32[512,20,64]{0,2,1:T(8,128)} %reshape.123, f32[512,20,64]{0,2,1:T(8,128)} %bitcast.124, f32[20]{0:T(128)S(1)} %copy-done.12, f32[512,20,64]{0,2,1:T(8,128)S(1)} %bitcast.122, f32[512,20]{0,1:T(8,128)S(1)} %bitcast.133, f32[20,64,512]{2,1,0:T(8,128)S(1)} %fusion.26), kind=kLoop, calls=%fused_computation.36 | loop fusion | flops 7208448 | bytes 13150288 | tf_op jit(solution)/shard_map/reduce_sum | solution.py:122
  161.7 3.2 %copy.78 = f32[512,1280]{1,0:T(8,128)} copy(f32[512,1280]{0,1:T(8,128)} %bitcast.123) | data formatting | bytes 5242880 | tf_op jit(solution)/shard_map/reshape | solution.py:119
  164.9 5.7 %psum.7 = f32[512]{0:T(512)S(1)} all-reduce(f32[512]{0:T(512)S(1)} %get-tuple-element.186), channel_id=1, replica_groups=mesh['ctx'=8,'grp'=4] {'grp'}, use_global_device_ids=true, to_apply=%region_9.10 | all-reduce | flops 512 | bytes 4096 | tf_op jit(solution)/shard_map/psum | solution.py:122
  170.6 2.6 %fusion.25 = bf16[512,1280]{1,0:T(8,128)(2,1)S(1)} fusion(f32[512,1280]{1,0:T(8,128)} %copy.78, bf16[128,4,1280]{2,0,1:T(8,128)(2,1)S(1)} %copy.77, f32[1280]{0:T(1024)S(1)} %copy-done.11, f32[512]{0:T(512)S(1)} %add_rsqrt_fusion), kind=kLoop, calls=%fused_computation.37 | loop fusion | flops 5898240 | bytes 5250048 | tf_op jit(solution)/shard_map/convert_element_type | solution.py:124
  173.2 7.7 %convolution_convert_fusion = bf16[512,2560]{1,0:T(8,128)(2,1)} fusion(bf16[512,1280]{1,0:T(8,128)(2,1)S(1)} %fusion.25, bf16[1280,2560]{1,0:T(8,128)(2,1)} %param.21), kind=kOutput, calls=%fused_computation.17 | convolution fusion | flops 3356753920 | bytes 10485760 | tf_op jit(solution)/shard_map/dot_general | solution.py:126
  180.9 33.4 %reduce-scatter.2.cloned.1.call-done = bf16[128,2560]{1,0:T(8,128)(2,1)} async-done(((bf16[512,2560]{1,0:T(8,128)(2,1)}), bf16[128,2560]{1,0:T(8,128)(2,1)}) %reduce-scatter.2.cloned.1.call-update) | async-done | bytes 655376 | tf_op jit(solution)/shard_map/reduce_scatter | solution.py:125
  (91 shorter events, 13.3 us)
Async XLA Ops:
  6.5 4.5 %copy-start.9 = (bf16[128,80]{0,1:T(8,128)(2,1)S(1)}, bf16[128,80]{0,1:T(8,128)(2,1)}, u32[]{:S(2)}) copy-start(bf16[128,80]{0,1:T(8,128)(2,1)} %param.18) | copy-start | bytes 61444
  6.5 8.8 %copy-start.8 = (bf16[128,128]{1,0:T(8,128)(2,1)S(1)}, bf16[128,128]{1,0:T(8,128)(2,1)}, u32[]{:S(2)}) copy-start(bf16[128,128]{1,0:T(8,128)(2,1)} %param.15) | copy-start | bytes 98308
  6.5 21.6 %copy-start.10 = (bf16[128,80]{0,1:T(8,128)(2,1)S(1)}, bf16[128,80]{0,1:T(8,128)(2,1)}, u32[]{:S(2)}) copy-start(bf16[128,80]{0,1:T(8,128)(2,1)} %param.17) | copy-start | bytes 61444
  7.9 28.1 %collective-permute-start = (bf16[128,1280]{1,0:T(8,128)(2,1)S(1)}, bf16[128,1280]{1,0:T(8,128)(2,1)}, u32[]{:S(2)}, u32[]{:S(2)}) collective-permute-start(bf16[128,1280]{1,0:T(8,128)(2,1)S(1)} %get-tuple-element.191), channel_id=1, source_target_pairs={{0,1},{1,0},{2,3},{3,2},{4,5},{5,4},{6,7},{7,6},{8,9},{9,8},{10,11... | collective-permute-start | bytes 983048 | tf_op jit(solution)/shard_map/ppermute | solution.py:23
  8.4 28.9 %collective-permute-start.1 = (bf16[128,1280]{1,0:T(8,128)(2,1)S(1)}, bf16[128,1280]{1,0:T(8,128)(2,1)}, u32[]{:S(2)}, u32[]{:S(2)}) collective-permute-start(bf16[128,1280]{1,0:T(8,128)(2,1)S(1)} %get-tuple-element.193), channel_id=1, source_target_pairs={{0,2},{1,3},{2,0},{3,1},{4,6},{5,7},{6,4},{7,5},{8,10},{9,11},{10,... | collective-permute-start | bytes 983048 | tf_op jit(solution)/shard_map/ppermute | solution.py:23
  11.0 27.6 %collective-permute-start.2 = (bf16[128,1280]{1,0:T(8,128)(2,1)S(1)}, bf16[128,1280]{1,0:T(8,128)(2,1)}, u32[]{:S(2)}, u32[]{:S(2)}) collective-permute-start(bf16[128,1280]{1,0:T(8,128)(2,1)S(1)} %get-tuple-element.190), channel_id=1, source_target_pairs={{0,3},{1,2},{2,1},{3,0},{4,7},{5,6},{6,5},{7,4},{8,11},{9,10},{10,... | collective-permute-start | bytes 983048 | tf_op jit(solution)/shard_map/ppermute | solution.py:23
  11.7 17.1 %all-to-all-start.1 = ((bf16[128,4,20]{0,2,1:T(8,128)(2,1)}), bf16[128,4,20]{0,2,1:T(8,128)(2,1)S(1)}, u32[]{:S(2)}, u32[]{:S(2)}) async-start(bf16[128,4,20]{0,2,1:T(8,128)(2,1)} %all_to_all.32), calls=%async_computation.1 | async-start | bytes 49152 | tf_op jit(solution)/shard_map/all_to_all | solution.py:95
  28.7 7.2 %all-to-all-start = ((bf16[128,4,20]{0,2,1:T(8,128)(2,1)}), bf16[128,4,20]{0,2,1:T(8,128)(2,1)S(1)}, u32[]{:S(2)}, u32[]{:S(2)}) async-start(bf16[128,4,20]{0,2,1:T(8,128)(2,1)} %all_to_all.30), calls=%async_computation | async-start | bytes 49152 | tf_op jit(solution)/shard_map/all_to_all | solution.py:94
  32.0 108.5 %all-gather.4.cloned.1.call-start = ((), (), s32[]{:S(2)}) async-start(), calls=%async_computation.5 | async-start | bytes 5898240 | tf_op jit(solution)/shard_map/all_gather | solution.py:30
  33.8 2.3 %copy-start.4 = (f32[2,20,256]{2,0,1:T(2,128)}, f32[2,20,256]{2,0,1:T(2,128)S(1)}, u32[]{:S(2)}) copy-start(f32[2,20,256]{2,0,1:T(2,128)S(1)} %reduce_window_sum.35) | copy-start | bytes 122884
  38.6 4.0 %copy-start.6 = (f32[2,256,20]{1,0,2:T(2,128)S(1)}, f32[2,256,20]{1,0,2:T(2,128)}, u32[]{:S(2)}) copy-start(f32[2,256,20]{1,0,2:T(2,128)} %get-tuple-element.197) | copy-start | bytes 122884
  51.1 0.8 copy-start
  52.0 6.1 %copy-start.13 = (u32[32]{0:T(128)S(1)}, u32[32]{0:T(128)}, u32[]{:S(2)}) copy-start(u32[32]{0:T(128)} %constant.80) | copy-start | bytes 388
  54.4 66.8 %all-to-all-start.2 = ((bf16[128,4,1280]{0,2,1:T(8,128)(2,1)}), bf16[128,4,1280]{0,2,1:T(8,128)(2,1)S(1)}, u32[]{:S(2)}, u32[]{:S(2)}) async-start(bf16[128,4,1280]{0,2,1:T(8,128)(2,1)} %bitcast.125), calls=%async_computation.2 | async-start | bytes 2621440 | tf_op jit(solution)/shard_map/all_to_all | solution.py:93
  58.0 156.3 %reduce-scatter.2.cloned.1.call-start = ((), (), s32[]{:S(2)}) async-start(), calls=%async_computation.4 | async-start | bytes 3276800 | tf_op jit(solution)/shard_map/reduce_scatter | solution.py:125
  104.0 2.8 %copy-start.2 = (f32[2,256,20,64]{1,0,3,2:T(2,128)S(1)}, f32[2,256,20,64]{1,0,3,2:T(2,128)}, u32[]{:S(2)}) copy-start(f32[2,256,20,64]{1,0,3,2:T(2,128)} %get-tuple-element.189) | copy-start | bytes 7864324
  104.0 2.8 %copy-start.5 = (f32[2,256,256]{2,1,0:T(8,128)S(1)}, f32[2,256,256]{2,1,0:T(8,128)}, u32[]{:S(2)}) copy-start(f32[2,256,256]{2,1,0:T(8,128)} %fusion.30) | copy-start | bytes 1572868
  104.0 2.8 %copy-start.7 = (pred[256,256]{1,0:T(8,128)(4,1)S(1)}, pred[256,256]{1,0:T(8,128)(4,1)}, u32[]{:S(2)}) copy-start(pred[256,256]{1,0:T(8,128)(4,1)} %iota_compare_fusion) | copy-start | bytes 196612
  106.8 11.2 %copy-start.3 = (f32[2,20,64,128]{3,2,1,0:T(8,128)S(1)}, f32[2,20,64,128]{3,2,1,0:T(8,128)}, u32[]{:S(2)}) copy-start(f32[2,20,64,128]{3,2,1,0:T(8,128)} %get-tuple-element.127) | copy-start | bytes 3932164
  154.3 1.7 copy-start.1
  154.3 1.7 copy-start.12
  161.7 8.9 %copy-start.11 = (f32[1280]{0:T(1024)S(1)}, f32[1280]{0:T(1024)}, u32[]{:S(2)}) copy-start(f32[1280]{0:T(1024)} %param.20) | copy-start | bytes 15364
Sparse Core Ops, SparseCore 0:
  52.1 88.3 all-gather.3
  181.0 33.1 reduce-scatter.1
